TPU v7x, 32 devices: a whole 2x2x4 slice. The times are simulated.
32 devices in a mesh: slot: 4 (over z), pb: 8 (over y, x, core).
Axes of the slice: x: 2, y: 2, z: 4, core: 2. Of those that a mesh axis runs over, the one named last changes fastest.
Arguments:
- inputs: bfloat16 [8, 4, 64, 1024], P('pb', 'slot'), may hold values from -6 to 6
- memory: bfloat16 [8, 4, 128, 1024], P('pb', 'slot'), may hold values from -6 to 6
- attn_weight: bfloat16 [1024, 6, 1024], P('pb'), may hold values from -0.1875 to 0.1875
- attn_out: bfloat16 [1024, 2, 1024], P('pb'), may hold values from -0.75 to 0.75
- ffn_in: bfloat16 [1024, 4096], P('pb'), may hold values from -0.1875 to 0.1875
- ffn_out: bfloat16 [4096, 1024], P('pb'), may hold values from -0.09375 to 0.09375
- attn_bias: float32 [1024, 6], replicated, may hold values from -3 to 3
- norm_gain: float32 [1024, 3], replicated, may hold values from 0.5 to 1.5
- norm_bias: float32 [1024, 3], replicated, may hold values from -2 to 2
- bias_in: float32 [4096], replicated, may hold values from -3 to 3
- bias_out: float32 [1024], replicated, may hold values from -2 to 2
- embedding: bfloat16 [32768, 1024], P('pb'), may hold values from -0.375 to 0.375
- targets: int32 [8, 64], replicated, may hold values from 0 to 32767
- slot_counts: int32 [8], replicated, may hold values from 2 to 4
- pad_mask: int32 [8, 64], P('pb'), may hold values 0 or 1
- log_prior: float32 [8, 4], P('pb', 'slot'), may hold values from -4 to 4
Outputs:
- token_logprob: float32 [8, 64], P('pb')
- grad_inputs: float32 [8, 4, 64, 1024], P('pb', 'slot')
- grad_memory: float32 [8, 4, 128, 1024], P('pb', 'slot')
- grad_log_prior: float32 [8, 4], P('pb', 'slot')
- grad_attn_weight: float32 [1024, 6, 1024], P(('slot', 'pb'))
- grad_attn_out: float32 [1024, 2, 1024], P(('slot', 'pb'))
- grad_ffn_in: float32 [1024, 4096], P(('slot', 'pb'))
- grad_ffn_out: float32 [4096, 1024], P(('slot', 'pb'))
- grad_attn_bias: float32 [1024, 6], P(('slot', 'pb'))
- grad_norm_gain: float32 [1024, 3], P(('slot', 'pb'))
- grad_norm_bias: float32 [1024, 3], P(('slot', 'pb'))
- grad_bias_in: float32 [4096], P(('slot', 'pb'))
- grad_bias_out: float32 [1024], P(('slot', 'pb'))
- grad_embedding: float32 [32768, 1024], P('pb')
Inputs may be any that keep to these rules, and one draw needn't show every extreme that they name: Slots 0 to slot_counts[q] - 1 of question q hold passages; the others are padding.
All inputs are finite; a program needn't handle non-finite values. No bound on the sum of `pad_mask` on one device may be relied on, other than what follows from the above.
Results may differ from a plain program's by a relative error of at most 0.029.
Values may be sent and summed in bfloat16 or wider, within the bound.
No kernel may reach another device: no remote copies, remote signals or barrier semaphores. Data moves between devices by JAX's collectives and lax.ppermute only.
A program may use at most 320 MiB of HBM per device.

v0:
```python
import jax
import jax.numpy as jnp
from jax import lax
from jax.sharding import PartitionSpec as P

HEAD = 64


def joined(value, axis, combine):
    everything = jax.tree.map(
        lambda part, kind: lax.all_gather(part.astype(kind), axis),
        value,
        (jnp.bfloat16, jnp.bfloat16, jnp.bfloat16),
    )

    def take(k):
        return jax.tree.map(lambda part, own: part[k].astype(own.dtype), everything, value)

    return lax.fori_loop(
        1, lax.axis_size(axis), lambda k, so_far: combine(so_far, take(k)), take(0)
    )


def merged(part, axis, combine):
    gathered = jax.tree.map(lambda a: lax.all_gather(a, axis), part)

    def take(source):
        return jax.tree.map(lambda a: lax.dynamic_index_in_dim(a, source, 0, False), gathered)

    return lax.fori_loop(
        1, lax.axis_size(axis), lambda source, state: combine(state, take(source)), take(0)
    )


def layer_norm(tensor, gain_row, shift_row):
    centered = tensor - jnp.mean(tensor, axis=-1, keepdims=True)
    variance = jnp.mean(centered * centered, axis=-1, keepdims=True)
    return centered * lax.rsqrt(variance + 1e-05) * gain_row + shift_row


def exact_gelu(tensor):
    return jax.nn.gelu(tensor, approximate=False)


def forward_product(activation, matrix):
    return jnp.dot(activation, matrix, preferred_element_type=jnp.float32)


def backward_product(gradient, matrix):
    return jnp.einsum("re,de->rd", gradient, matrix, preferred_element_type=jnp.float32)


def weight_product(activation, gradient):
    return jnp.einsum("rd,re->de", activation, gradient, preferred_element_type=jnp.float32)


def column_total(gradient):
    return jnp.sum(gradient.astype(jnp.float32), axis=0)


def split_heads(tensor):
    return tensor.reshape(tensor.shape[0], tensor.shape[1] // HEAD, HEAD)


def attend(queries, key_rows, value_rows, causal):
    query_heads = split_heads(queries)
    key_heads = split_heads(key_rows)
    value_heads = split_heads(value_rows)
    scores = (
        jnp.einsum("qhd,khd->hqk", query_heads, key_heads, preferred_element_type=jnp.float32)
        * 0.125
    )
    if causal:
        causal_keep = jnp.arange(scores.shape[1])[:, None] >= jnp.arange(scores.shape[2])[None, :]
        scores = jnp.where(causal_keep[None, :, :], scores, -1e30)
    attn_probs = jax.nn.softmax(scores, axis=-1)
    blended = jnp.einsum(
        "hqk,khd->qhd",
        attn_probs.astype(jnp.bfloat16),
        value_heads,
        preferred_element_type=jnp.float32,
    )
    return (blended.reshape(queries.shape[0], queries.shape[1]), attn_probs)


def attend_back(grad_low, queries, key_rows, value_rows, attn_probs):
    width = queries.shape[1]
    grad_heads = split_heads(grad_low)
    query_heads = split_heads(queries)
    key_heads = split_heads(key_rows)
    value_heads = split_heads(value_rows)
    grad_probs = jnp.einsum(
        "qhd,khd->hqk", grad_heads, value_heads, preferred_element_type=jnp.float32
    )
    grad_values = jnp.einsum(
        "hqk,qhd->khd",
        attn_probs.astype(jnp.bfloat16),
        grad_heads,
        preferred_element_type=jnp.float32,
    )
    centred = grad_probs - jnp.sum(grad_probs * attn_probs, axis=-1, keepdims=True)
    grad_scores = (attn_probs * centred).astype(jnp.bfloat16)
    grad_queries = (
        jnp.einsum("hqk,khd->qhd", grad_scores, key_heads, preferred_element_type=jnp.float32)
        * 0.125
    )
    grad_keys = (
        jnp.einsum("hqk,qhd->khd", grad_scores, query_heads, preferred_element_type=jnp.float32)
        * 0.125
    )
    return (
        grad_queries.reshape(-1, width).astype(jnp.bfloat16),
        grad_keys.reshape(-1, width).astype(jnp.bfloat16),
        grad_values.reshape(-1, width).astype(jnp.bfloat16),
    )


def combine_vocab(earlier, later):
    highest = jnp.maximum(earlier[0], later[0])
    summed = earlier[1] * jnp.exp(earlier[0] - highest) + later[1] * jnp.exp(later[0] - highest)
    return (highest, summed, earlier[2] + later[2])


def combine_slots(earlier, later):
    highest = jnp.maximum(earlier[0], later[0])
    summed = earlier[1] * jnp.exp(earlier[0] - highest) + later[1] * jnp.exp(later[0] - highest)
    return (highest, summed)


def shards(
    inputs,
    memory,
    attn_weight,
    attn_out,
    ffn_in,
    ffn_out,
    attn_bias,
    norm_gain,
    norm_bias,
    bias_in,
    bias_out,
    embedding,
    targets,
    slot_counts,
    pad_mask,
    log_prior,
):
    w_attn, w_out, w_up, w_down = (
        lax.all_gather(attn_weight, "pb", axis=0, tiled=True),
        lax.all_gather(attn_out, "pb", axis=0, tiled=True),
        lax.all_gather(ffn_in, "pb", axis=0, tiled=True),
        lax.all_gather(ffn_out, "pb", axis=0, tiled=True),
    )
    source = inputs[0, 0]
    passage = memory[0, 0]
    row_count = source.shape[0]
    queries = (forward_product(source, w_attn[:, 0, :]) + attn_bias[:, 0]).astype(jnp.bfloat16)
    key_rows = forward_product(source, w_attn[:, 1, :]).astype(jnp.bfloat16)
    value_rows = (forward_product(source, w_attn[:, 2, :]) + attn_bias[:, 1]).astype(jnp.bfloat16)
    self_mix, self_probs = attend(queries, key_rows, value_rows, True)
    self_low = self_mix.astype(jnp.bfloat16)
    resid_one = (
        source.astype(jnp.float32) + forward_product(self_low, w_out[:, 0, :]) + attn_bias[:, 2]
    )
    hidden_one, norm_back_one = jax.vjp(layer_norm, resid_one, norm_gain[:, 0], norm_bias[:, 0])
    hidden_one_low = hidden_one.astype(jnp.bfloat16)
    cross_queries = (forward_product(hidden_one_low, w_attn[:, 3, :]) + attn_bias[:, 3]).astype(
        jnp.bfloat16
    )
    cross_keys = forward_product(passage, w_attn[:, 4, :]).astype(jnp.bfloat16)
    cross_values = (forward_product(passage, w_attn[:, 5, :]) + attn_bias[:, 4]).astype(
        jnp.bfloat16
    )
    cross_mix, cross_probs = attend(cross_queries, cross_keys, cross_values, False)
    cross_low = cross_mix.astype(jnp.bfloat16)
    resid_two = hidden_one + forward_product(cross_low, w_out[:, 1, :]) + attn_bias[:, 5]
    hidden_two, norm_back_two = jax.vjp(layer_norm, resid_two, norm_gain[:, 1], norm_bias[:, 1])
    hidden_two_low = hidden_two.astype(jnp.bfloat16)
    upward = forward_product(hidden_two_low, w_up) + bias_in
    active, gelu_back = jax.vjp(exact_gelu, upward)
    active_low = active.astype(jnp.bfloat16)
    resid_three = hidden_two + forward_product(active_low, w_down) + bias_out
    hidden_three, norm_back_three = jax.vjp(
        layer_norm, resid_three, norm_gain[:, 2], norm_bias[:, 2]
    )
    final_low = hidden_three.astype(jnp.bfloat16)
    final_all = lax.all_gather(final_low, "pb", axis=0, tiled=True)
    vocab_rows = embedding.shape[0]
    question = lax.axis_index("pb")
    local_ids = targets.reshape(-1) - question * vocab_rows
    target_hit = local_ids[:, None] == jnp.arange(vocab_rows)[None, :]
    scores_kept = jnp.einsum("td,vd->tv", final_all, embedding, preferred_element_type=jnp.float32)
    block_peak = jnp.max(scores_kept, axis=1)
    block_total = jnp.sum(jnp.exp(scores_kept - block_peak[:, None]), axis=1)
    block_pick = jnp.sum(jnp.where(target_hit, scores_kept, 0.0), axis=1)
    peak_all, total_all, pick_all = joined(
        (block_peak, block_total, block_pick), "pb", combine_vocab
    )
    norm_all = peak_all + jnp.log(total_all)
    first_row = question * row_count
    own_norm = lax.dynamic_slice_in_dim(norm_all, first_row, row_count)
    own_pick = lax.dynamic_slice_in_dim(pick_all, first_row, row_count)
    slot_logp = own_pick - own_norm + log_prior[0, 0]
    usable = lax.axis_index("slot") < slot_counts[question]
    masked_logp = jnp.where(usable, slot_logp, -1e30)
    presence = jnp.where(usable, 1.0, 0.0) * jnp.ones_like(slot_logp)
    slot_peak, slot_total = merged((masked_logp, presence), "slot", combine_slots)
    token_logprob = slot_peak + jnp.log(slot_total)
    posterior = jnp.exp(masked_logp - token_logprob)
    token_grad = -pad_mask[0].astype(jnp.float32) * posterior
    prior_grad = jnp.sum(token_grad).reshape(1, 1)
    grad_tokens_all = lax.all_gather(token_grad, "pb", axis=0, tiled=True)
    vocab_soft = jnp.exp(scores_kept - norm_all[:, None])
    logit_grad = (grad_tokens_all[:, None] * (jnp.where(target_hit, 1.0, 0.0) - vocab_soft)).astype(
        jnp.bfloat16
    )
    embed_part = jnp.einsum("tv,td->vd", logit_grad, final_all, preferred_element_type=jnp.float32)
    grad_embedding = lax.psum(embed_part.astype(jnp.bfloat16), "slot").astype(jnp.float32)
    grad_final = lax.psum_scatter(
        jnp.dot(logit_grad, embedding, preferred_element_type=jnp.float32),
        "pb",
        scatter_dimension=0,
        tiled=True,
    )
    grad_resid_three, gain_three, shift_three = norm_back_three(grad_final)
    branch_three = grad_resid_three.astype(jnp.bfloat16)
    grad_down = weight_product(active_low, branch_three)
    grad_bias_out = column_total(branch_three)
    grad_active = backward_product(branch_three, w_down).astype(jnp.bfloat16)
    grad_upward = gelu_back(grad_active.astype(jnp.float32))[0].astype(jnp.bfloat16)
    grad_up = weight_product(hidden_two_low, grad_upward)
    grad_bias_in = column_total(grad_upward)
    grad_hidden_two = grad_resid_three + backward_product(grad_upward, w_up)
    grad_resid_two, gain_two, shift_two = norm_back_two(grad_hidden_two)
    branch_two = grad_resid_two.astype(jnp.bfloat16)
    grad_cross_out = weight_product(cross_low, branch_two)
    bias_cross_out = column_total(branch_two)
    grad_cross_mix = backward_product(branch_two, w_out[:, 1, :]).astype(jnp.bfloat16)
    cross_query_grad, cross_key_grad, cross_value_grad = attend_back(
        grad_cross_mix, cross_queries, cross_keys, cross_values, cross_probs
    )
    grad_hidden_one = grad_resid_two + backward_product(cross_query_grad, w_attn[:, 3, :])
    grad_passage = backward_product(cross_key_grad, w_attn[:, 4, :]) + backward_product(
        cross_value_grad, w_attn[:, 5, :]
    )
    grad_resid_one, gain_one, shift_one = norm_back_one(grad_hidden_one)
    branch_one = grad_resid_one.astype(jnp.bfloat16)
    grad_self_out = weight_product(self_low, branch_one)
    bias_self_out = column_total(branch_one)
    grad_self_mix = backward_product(branch_one, w_out[:, 0, :]).astype(jnp.bfloat16)
    self_query_grad, self_key_grad, self_value_grad = attend_back(
        grad_self_mix, queries, key_rows, value_rows, self_probs
    )
    grad_source = (
        grad_resid_one
        + backward_product(self_query_grad, w_attn[:, 0, :])
        + backward_product(self_key_grad, w_attn[:, 1, :])
        + backward_product(self_value_grad, w_attn[:, 2, :])
    )
    grad_attn = jnp.stack(
        [
            weight_product(source, self_query_grad),
            weight_product(source, self_key_grad),
            weight_product(source, self_value_grad),
            weight_product(hidden_one_low, cross_query_grad),
            weight_product(passage, cross_key_grad),
            weight_product(passage, cross_value_grad),
        ],
        axis=1,
    )
    grad_outputs = jnp.stack([grad_self_out, grad_cross_out], axis=1)
    grad_biases = jnp.stack(
        [
            column_total(self_query_grad),
            column_total(self_value_grad),
            bias_self_out,
            column_total(cross_query_grad),
            column_total(cross_value_grad),
            bias_cross_out,
        ],
        axis=1,
    )
    grad_gains = jnp.stack([gain_one, gain_two, gain_three], axis=1)
    grad_shifts = jnp.stack([shift_one, shift_two, shift_three], axis=1)
    (
        summed_attn,
        summed_outputs,
        summed_up,
        summed_down,
        summed_biases,
        summed_gains,
        summed_shifts,
        summed_bias_in,
        summed_bias_out,
    ) = (
        lax.psum_scatter(grad_attn, ("slot", "pb"), scatter_dimension=0, tiled=True),
        lax.psum_scatter(grad_outputs, ("slot", "pb"), scatter_dimension=0, tiled=True),
        lax.psum_scatter(grad_up, ("slot", "pb"), scatter_dimension=0, tiled=True),
        lax.psum_scatter(grad_down, ("slot", "pb"), scatter_dimension=0, tiled=True),
        lax.psum_scatter(grad_biases, ("slot", "pb"), scatter_dimension=0, tiled=True),
        lax.psum_scatter(grad_gains, ("slot", "pb"), scatter_dimension=0, tiled=True),
        lax.psum_scatter(grad_shifts, ("slot", "pb"), scatter_dimension=0, tiled=True),
        lax.psum_scatter(grad_bias_in, ("slot", "pb"), scatter_dimension=0, tiled=True),
        lax.psum_scatter(grad_bias_out, ("slot", "pb"), scatter_dimension=0, tiled=True),
    )
    return (
        token_logprob[None, :],
        grad_source[None, None],
        grad_passage[None, None],
        prior_grad,
        summed_attn,
        summed_outputs,
        summed_up,
        summed_down,
        summed_biases,
        summed_gains,
        summed_shifts,
        summed_bias_in,
        summed_bias_out,
        grad_embedding,
    )


def solution(mesh):
    placed = (
        P("pb", "slot", None, None),
        P("pb", "slot", None, None),
        P("pb", None, None),
        P("pb", None, None),
        P("pb", None),
        P("pb", None),
        P(),
        P(),
        P(),
        P(),
        P(),
        P("pb", None),
        P(),
        P(),
        P("pb", None),
        P("pb", "slot"),
    )
    return jax.shard_map(
        shards,
        mesh=mesh,
        in_specs=placed,
        out_specs=(
            P("pb", None),
            P("pb", "slot", None, None),
            P("pb", "slot", None, None),
            P("pb", "slot"),
            P(("slot", "pb"), None, None),
            P(("slot", "pb"), None, None),
            P(("slot", "pb"), None),
            P(("slot", "pb"), None),
            P(("slot", "pb"), None),
            P(("slot", "pb"), None),
            P(("slot", "pb"), None),
            P(("slot", "pb")),
            P(("slot", "pb")),
            P("pb", None),
        ),
        check_vma=False,
    )
```

profile of v0, /device:TPU:2, one launch (start us, length us, event | category | flops | bytes accessed | tf_op | source)
XLA Modules:
  0.0 2007.9 jit_solution(12567964472854483970)
XLA Ops:
  15.2 68.1 %all-gather.13.cloned.1.call-done = bf16[1024,6,1024]{2,0,1:T(8,128)(2,1)} async-done(((bf16[128,6,1024]{2,0,1:T(8,128)(2,1)}), bf16[1024,6,1024]{2,0,1:T(8,128)(2,1)}) %all-gather.13.cloned.1.call-update) | async-done | bytes 12582928 | tf_op jit(solution)/shard_map/all_gather | solution.py:149
  93.9 28.6 %all-gather.15.cloned.1.call-done = bf16[1024,2,1024]{2,0,1:T(8,128)(2,1)} async-done(((bf16[128,2,1024]{2,0,1:T(8,128)(2,1)}), bf16[1024,2,1024]{2,0,1:T(8,128)(2,1)}) %all-gather.15.cloned.1.call-update) | async-done | bytes 4194320 | tf_op jit(solution)/shard_map/all_gather | solution.py:150
  134.5 44.5 %all-gather.17.cloned.1.call-done = bf16[1024,4096]{1,0:T(8,128)(2,1)} async-done(((bf16[128,4096]{1,0:T(8,128)(2,1)}), bf16[1024,4096]{1,0:T(8,128)(2,1)}) %all-gather.17.cloned.1.call-update) | async-done | bytes 8388624 | tf_op jit(solution)/shard_map/all_gather | solution.py:151
  185.1 50.0 %all-gather.19.cloned.1.call-done = bf16[4096,1024]{1,0:T(8,128)(2,1)} async-done(((bf16[512,1024]{1,0:T(8,128)(2,1)}), bf16[4096,1024]{1,0:T(8,128)(2,1)}) %all-gather.19.cloned.1.call-update) | async-done | bytes 8388624 | tf_op jit(solution)/shard_map/all_gather | solution.py:152
  248.8 18.2 all-gather.21.cloned.1.call-done
  285.3 8.9 all-gather.5
  303.0 11.7 all-reduce.6
  316.3 10.1 all-reduce.2
  333.5 8.2 fusion.113
  342.2 39.8 %reduce-scatter.15.cloned.1.call-done = f32[64,1024]{1,0:T(8,128)} async-done(((f32[512,1024]{1,0:T(8,128)}), f32[64,1024]{1,0:T(8,128)}) %reduce-scatter.15.cloned.1.call-update) | async-done | bytes 262160 | tf_op jit(solution)/shard_map/reduce_scatter | solution.py:219
  385.6 8.7 convert_reduce_fusion
  437.2 10.5 convolution_convert_fusion
  473.0 29.7 %copy.130 = f32[1024,6,1024]{2,1,0:T(8,128)} copy(f32[1024,6,1024]{0,2,1:T(8,128)} %bitcast_dynamic-update-slice_fusion) | data formatting | bytes 50331648 | tf_op jit(solution)/shard_map/stack | solution.py:260
  503.3 8.1 fusion.93
  512.4 11.1 fusion.98
  524.2 40.5 %all-reduce.5 = (f32[4096]{0:T(1024)S(1)}, f32[1024]{0:T(1024)S(1)}) all-reduce(f32[4096]{0:T(1024)S(1)} %copy-done.35, f32[1024]{0:T(1024)S(1)} %copy-done.33), channel_id=15, replica_groups=mesh['slot'=4,'pb'=8] {'slot','pb'}, use_global_device_ids=true, to_apply=%region_47.48.clone | all-reduce | flops 5120 | bytes 40960
  580.7 109.8 %reduce-scatter.29.cloned.1.call-done = f32[32,3]{1,0:T(8,128)} async-done(((f32[1024,3]{1,0:T(8,128)}), f32[32,3]{1,0:T(8,128)}) %reduce-scatter.29.cloned.1.call-update) | async-done | bytes 400
  691.8 131.6 %reduce-scatter.25.cloned.1.call-done = f32[32,6]{1,0:T(8,128)} async-done(((f32[1024,6]{1,0:T(8,128)}), f32[32,6]{1,0:T(8,128)}) %reduce-scatter.25.cloned.1.call-update) | async-done | bytes 784
  824.8 293.7 %all-reduce.9.cloned.1.call-done = bf16[4096,1024]{1,0:T(8,128)(2,1)} async-done(((bf16[4096,1024]{1,0:T(8,128)(2,1)}), bf16[4096,1024]{1,0:T(8,128)(2,1)}) %all-reduce.9.cloned.1.call-update) | async-done | bytes 8388624 | tf_op jit(solution)/shard_map/psum | solution.py:218
  1118.5 11.7 convert_element_type.365
  1130.2 132.8 %reduce-scatter.19.cloned.1.call-done = f32[32,2,1024]{2,0,1:T(8,128)} async-done(((f32[1024,2,1024]{2,0,1:T(8,128)}), f32[32,2,1024]{2,0,1:T(8,128)}) %reduce-scatter.19.cloned.1.call-update) | async-done | bytes 262160 | tf_op jit(solution)/shard_map/reduce_scatter | solution.py:297
  1264.8 359.8 %reduce-scatter.17.cloned.1.call-done = f32[32,6,1024]{2,1,0:T(8,128)} async-done(((f32[1024,6,1024]{2,1,0:T(8,128)}), f32[32,6,1024]{2,1,0:T(8,128)}) %reduce-scatter.17.cloned.1.call-update) | async-done | bytes 786448 | tf_op jit(solution)/shard_map/reduce_scatter | solution.py:296
  1627.2 186.5 %reduce-scatter.21.cloned.1.call-done = f32[32,4096]{1,0:T(8,128)} async-done(((f32[1024,4096]{1,0:T(8,128)}), f32[32,4096]{1,0:T(8,128)}) %reduce-scatter.21.cloned.1.call-update) | async-done | bytes 524304 | tf_op jit(solution)/shard_map/reduce_scatter | solution.py:298
  1813.7 187.2 %reduce-scatter.23.cloned.1.call-done = f32[128,1024]{1,0:T(8,128)} async-done(((f32[4096,1024]{1,0:T(8,128)}), f32[128,1024]{1,0:T(8,128)}) %reduce-scatter.23.cloned.1.call-update) | async-done | bytes 524304 | tf_op jit(solution)/shard_map/reduce_scatter | solution.py:299
  (302 shorter events, 180.7 us)
Async XLA Ops:
  7.2 76.2 %copy-start = (bf16[1,1,128,1024]{3,2,1,0:T(8,128)(2,1)S(1)}, bf16[1,1,128,1024]{3,2,1,0:T(8,128)(2,1)}, u32[]{:S(2)}) copy-start(bf16[1,1,128,1024]{3,2,1,0:T(8,128)(2,1)} %param.21) | copy-start | bytes 786436
  7.2 78.4 %copy-start.4 = (bf16[1,1,64,1024]{3,2,1,0:T(8,128)(2,1)S(1)}, bf16[1,1,64,1024]{3,2,1,0:T(8,128)(2,1)}, u32[]{:S(2)}) copy-start(bf16[1,1,64,1024]{3,2,1,0:T(8,128)(2,1)} %param.20) | copy-start | bytes 393220
  7.2 76.1 %all-gather.13.cloned.1.call-start = ((), (), s32[]{:S(2)}) async-start(), calls=%async_computation.8 | async-start | bytes 14155776 | tf_op jit(solution)/shard_map/all_gather | solution.py:149
  7.9 114.6 %all-gather.15.cloned.1.call-start = ((), (), s32[]{:S(2)}) async-start(), calls=%async_computation.9 | async-start | bytes 4718592 | tf_op jit(solution)/shard_map/all_gather | solution.py:150
  10.0 169.0 %all-gather.17.cloned.1.call-start = ((), (), s32[]{:S(2)}) async-start(), calls=%async_computation.10 | async-start | bytes 9437184 | tf_op jit(solution)/shard_map/all_gather | solution.py:151
  10.7 224.4 %all-gather.19.cloned.1.call-start = ((), (), s32[]{:S(2)}) async-start(), calls=%async_computation.11 | async-start | bytes 9437184 | tf_op jit(solution)/shard_map/all_gather | solution.py:152
  11.3 255.8 %all-gather.21.cloned.1.call-start = ((), (), s32[]{:S(2)}) async-start(), calls=%async_computation.12 | async-start | bytes 1179648 | tf_op jit(solution)/shard_map/all_gather | solution.py:187
  12.8 112.2 %copy-start.24 = (f32[1024,1]{0,1:T(1,128)}, f32[1024,1]{0,1:T(1,128)S(1)}, u32[]{:S(2)}) copy-start(f32[1024,1]{0,1:T(1,128)S(1)} %get-tuple-element.457) | copy-start | bytes 12292
  134.2 100.9 %copy-start.48 = (f32[1024]{0:T(1024)S(1)}, f32[1024]{0:T(1024)}, u32[]{:S(2)}) copy-start(f32[1024]{0:T(1024)} %param.30) | copy-start | bytes 12292
  134.2 108.1 %copy-start.28 = (f32[64]{0:T(128)}, f32[64]{0:T(128)S(1)}, u32[]{:S(2)}) copy-start(f32[64]{0:T(128)S(1)} %broadcast_multiply_fusion.1) | copy-start | bytes 772
  134.5 107.9 %copy-start.30 = (f32[64]{0:T(128)}, f32[64]{0:T(128)S(1)}, u32[]{:S(2)}) copy-start(f32[64]{0:T(128)S(1)} %fusion.88) | copy-start | bytes 772
  185.0 59.0 %copy-start.40 = (s32[8,64]{1,0:T(8,128)S(1)}, s32[8,64]{1,0:T(8,128)}, u32[]{:S(2)}) copy-start(s32[8,64]{1,0:T(8,128)} %param.32) | copy-start | bytes 6148
  185.0 59.1 %copy-start.51 = (u32[32]{0:T(128)S(1)}, u32[32]{0:T(128)}, u32[]{:S(2)}) copy-start(u32[32]{0:T(128)} %constant.196) | copy-start | bytes 388
  185.0 59.7 %copy-start.50 = (u32[32]{0:T(128)S(1)}, u32[32]{0:T(128)}, u32[]{:S(2)}) copy-start(u32[32]{0:T(128)} %constant.206) | copy-start | bytes 388
  185.1 61.6 %copy-start.49 = (s32[8]{0:T(128)S(1)}, s32[8]{0:T(128)}, u32[]{:S(2)}) copy-start(s32[8]{0:T(128)} %param.33) | copy-start | bytes 100
  243.3 138.7 %reduce-scatter.15.cloned.1.call-start = ((), (), s32[]{:S(2)}) async-start(), calls=%async_computation.13 | async-start | bytes 2359296 | tf_op jit(solution)/shard_map/reduce_scatter | solution.py:219
  341.8 237.6 %reduce-scatter.27.cloned.1.call-start = ((), (), s32[]{:S(2)}) async-start(), calls=%async_computation.20 | async-start | bytes 540672
  429.7 260.8 %reduce-scatter.29.cloned.1.call-start = ((), (), s32[]{:S(2)}) async-start(), calls=%async_computation.21 | async-start | bytes 540672
  431.5 391.9 %reduce-scatter.25.cloned.1.call-start = ((), (), s32[]{:S(2)}) async-start(), calls=%async_computation.19 | async-start | bytes 540672
  437.2 681.3 %all-reduce.9.cloned.1.call-start = ((), (), s32[]{:S(2)}) async-start(), calls=%async_computation.18 | async-start | bytes 16777216 | tf_op jit(solution)/shard_map/psum | solution.py:218
  447.8 815.2 %reduce-scatter.19.cloned.1.call-start = ((), (), s32[]{:S(2)}) async-start(), calls=%async_computation.15 | async-start | bytes 8650752 | tf_op jit(solution)/shard_map/reduce_scatter | solution.py:297
  454.2 1170.5 %reduce-scatter.17.cloned.1.call-start = ((), (), s32[]{:S(2)}) async-start(), calls=%async_computation.14 | async-start | bytes 34603008 | tf_op jit(solution)/shard_map/reduce_scatter | solution.py:296
  502.7 1311.0 %reduce-scatter.21.cloned.1.call-start = ((), (), s32[]{:S(2)}) async-start(), calls=%async_computation.16 | async-start | bytes 17301504 | tf_op jit(solution)/shard_map/reduce_scatter | solution.py:298
  511.5 1489.4 %reduce-scatter.23.cloned.1.call-start = ((), (), s32[]{:S(2)}) async-start(), calls=%async_computation.17 | async-start | bytes 17301504 | tf_op jit(solution)/shard_map/reduce_scatter | solution.py:299
  (42 other events, 611.2 us)
Sparse Core Ops, SparseCore 0:
  9.9 73.3 all-gather.12
  85.8 36.7 all-gather.14
  124.5 54.4 all-gather.16
  180.7 54.3 all-gather.18
  243.5 23.5 all-gather.20
  341.9 40.1 reduce-scatter.14
  429.8 128.5 reduce-scatter.26
  560.6 129.8 reduce-scatter.28
  693.4 129.9 reduce-scatter.24
  826.3 292.1 all-reduce.8
  1120.8 142.1 reduce-scatter.18
  1265.1 359.4 reduce-scatter.16
  1627.5 186.1 reduce-scatter.20
  1816.4 184.4 reduce-scatter.22
where the time goes:
time: 2020 us; the launch traced here: 2010 us
  waiting for transfers between devices  1650 us (82%)
  matrix products  142 us (7%)
  blocking collectives  87.1 us (4%)
  local copies, waits for them, and re-layouts  68.3 us (3%)
  other arithmetic  38 us (2%)
    reduce_scatter x1, waiting for transfers between devices, shards(): lax.psum_scatter(grad_attn, ('slot', 'pb'), scatter_dimension=0, tiled=True)  360 us
    psum x1, waiting for transfers between devices, shards(): lax.psum(embed_part.astype(jnp.bfloat16), 'slot').astype(jnp.float32)  294 us
    unnamed x17, waiting for transfers between devices  243 us
    reduce_scatter x1, waiting for transfers between devices, shards(): lax.psum_scatter(grad_down, ('slot', 'pb'), scatter_dimension=0, tiled=True)  187 us
    reduce_scatter x1, waiting for transfers between devices, shards(): lax.psum_scatter(grad_up, ('slot', 'pb'), scatter_dimension=0, tiled=True)  187 us
    reduce_scatter x1, waiting for transfers between devices, shards(): lax.psum_scatter(grad_outputs, ('slot', 'pb'), scatter_dimension=0, tiled...  133 us
    all_gather x1, waiting for transfers between devices, shards(): lax.all_gather(attn_weight, 'pb', axis=0, tiled=True)  68.1 us
    unnamed x3, blocking collectives  62.3 us
  transfers between devices with their start and end apart: 14, of which 13 were waited for; matrix products, arithmetic and copies ran while one was open for 8% of the time, Pallas kernels for 0%

commit v1 on v0

v1 whole, which is shorter than its diff:
```python
import jax
import jax.numpy as jnp
from jax import lax
from jax.sharding import PartitionSpec as P

HEAD = 64
CHIPS = 4
CORES = 2
TEAM = CHIPS * CORES
BF = jnp.bfloat16
F32 = jnp.float32


def chip_pairs(size, k):
    return [(i, (i // TEAM) * TEAM + ((i % TEAM) // CORES ^ k) * CORES + i % CORES) for i in range(size)]


def from_chip(x, k):
    return lax.ppermute(x, "pb", chip_pairs(lax.axis_size("pb"), k))


def from_core(x):
    return lax.ppermute(x, "pb", [(i, i ^ 1) for i in range(lax.axis_size("pb"))])


def from_slot(x, k):
    size = lax.axis_size("slot")
    return lax.ppermute(x, "slot", [(i, (i + k) % size) for i in range(size)])


def team_groups():
    size = lax.axis_size("pb")
    return [[g * TEAM + j for g in range(size // TEAM)] for j in range(TEAM)]


def product(a, b):
    return jnp.dot(a, b, preferred_element_type=F32)


def product_t(a, b):
    return jnp.einsum("re,de->rd", a, b, preferred_element_type=F32)


def weight_product(a, g):
    return jnp.einsum("rd,re->de", a, g, preferred_element_type=F32)


def at(x, index):
    return lax.dynamic_index_in_dim(x, index, 0, False)


def collect(x):
    return jnp.stack([x] + [from_chip(x, k) for k in range(1, CHIPS)])


def reduce_chips(parts):
    total = parts[0]
    for k in range(1, CHIPS):
        total = total + from_chip(parts[k].astype(BF), k).astype(F32)
    return total


def layer_norm(r, gain, shift):
    centered = r - jnp.mean(r, axis=-1, keepdims=True)
    inv = lax.rsqrt(jnp.mean(centered * centered, axis=-1, keepdims=True) + 1e-05)
    z = centered * inv
    return z * gain + shift, z, inv


def layer_norm_back(dh, z, inv, gain):
    dz = dh * gain
    dr = (dz - jnp.mean(dz, axis=-1, keepdims=True) - z * jnp.mean(dz * z, axis=-1, keepdims=True)) * inv
    return dr, jnp.sum(dh * z, axis=0), jnp.sum(dh, axis=0)


def exact_gelu(u):
    return jax.nn.gelu(u, approximate=False)


def heads(x, questions):
    return x.reshape(questions, x.shape[0] // questions, x.shape[1] // HEAD, HEAD)


def attend(q, k, v, questions, causal):
    qh, kh, vh = heads(q, questions), heads(k, questions), heads(v, questions)
    scores = jnp.einsum("bqhd,bkhd->bhqk", qh, kh, preferred_element_type=F32) * 0.125
    if causal:
        keep = jnp.arange(scores.shape[2])[:, None] >= jnp.arange(scores.shape[3])[None, :]
        scores = jnp.where(keep, scores, -1e30)
    probs = jax.nn.softmax(scores, axis=-1)
    mixed = jnp.einsum("bhqk,bkhd->bqhd", probs.astype(BF), vh, preferred_element_type=F32)
    return mixed.reshape(q.shape).astype(BF), probs


def attend_back(g, q, k, v, probs, questions):
    gh, qh, kh, vh = (heads(t, questions) for t in (g, q, k, v))
    dp = jnp.einsum("bqhd,bkhd->bhqk", gh, vh, preferred_element_type=F32)
    dv = jnp.einsum("bhqk,bqhd->bkhd", probs.astype(BF), gh, preferred_element_type=F32)
    ds = (probs * (dp - jnp.sum(dp * probs, axis=-1, keepdims=True))).astype(BF)
    dq = jnp.einsum("bhqk,bkhd->bqhd", ds, kh, preferred_element_type=F32) * 0.125
    dk = jnp.einsum("bhqk,bqhd->bkhd", ds, qh, preferred_element_type=F32) * 0.125
    return dq.reshape(q.shape).astype(BF), dk.reshape(k.shape).astype(BF), dv.reshape(v.shape).astype(BF)


def shards(
    inputs, memory, attn_weight, attn_out, ffn_in, ffn_out, attn_bias, norm_gain, norm_bias,
    bias_in, bias_out, embedding, targets, slot_counts, pad_mask, log_prior,
):
    n_pb, n_slot = lax.axis_size("pb"), lax.axis_size("slot")
    n_all = n_pb * n_slot
    teams = n_pb // TEAM
    me = lax.axis_index("pb")
    chip, core, team = (me % TEAM) // CORES, me % CORES, me // TEAM
    slot = lax.axis_index("slot")
    length, width = inputs.shape[2], inputs.shape[3]
    quarter = width // CHIPS

    def across_teams(w):
        return lax.all_gather(w, "pb", axis_index_groups=team_groups()) if teams > 1 else w[None]

    def natural(blocks):
        flat = blocks.reshape((TEAM,) + blocks.shape[2:])
        ordered = jnp.stack([at(flat, (core ^ c) * CHIPS + (chip ^ b)) for b in range(CHIPS) for c in range(CORES)])
        ordered = jnp.swapaxes(ordered, 0, 1)
        return ordered.reshape((-1,) + ordered.shape[3:])

    def column_shard(w):
        w = across_teams(w)
        pieces = jnp.moveaxis(w.reshape(w.shape[:-1] + (CHIPS, w.shape[-1] // CHIPS)), -2, 0)
        mine = [at(pieces, chip)]
        for k in range(1, CHIPS):
            mine.append(from_chip(at(pieces, chip ^ k), k))
        mine = jnp.stack(mine)
        return natural(jnp.stack([mine, from_core(mine)]))

    def all_rows(w):
        w = across_teams(w)
        mine = collect(w)
        return natural(jnp.stack([mine, from_core(mine)]))

    def chip_rows(w):
        other = from_core(w)
        pair = jnp.stack([w, other])
        return jnp.stack([at(pair, core), at(pair, 1 - core)]).reshape((-1,) + w.shape[1:])

    x_all = collect(inputs[0, 0]).reshape(CHIPS * length, width)
    w_cols = column_shard(attn_weight)
    m_all = collect(memory[0, 0]).reshape(-1, width)
    w_out = all_rows(attn_out)
    w_up = column_shard(ffn_in)
    if teams > 1:
        full_down = all_rows(ffn_out)
        w_down = lax.dynamic_slice_in_dim(full_down, chip * (full_down.shape[0] // CHIPS), full_down.shape[0] // CHIPS)
    else:
        w_down = chip_rows(ffn_out)
    out_mine = lax.dynamic_slice_in_dim(w_out, chip * quarter, quarter)

    def my_columns(b):
        return lax.dynamic_slice_in_dim(b, chip * (b.shape[0] // CHIPS), b.shape[0] // CHIPS)

    bias_cols = my_columns(attn_bias)

    def gather_columns(y):
        y = y.reshape(CHIPS, -1, y.shape[-1])
        got = []
        for k in range(CHIPS):
            r = from_chip(y, k) if k else y
            got.append(jnp.stack([r[k ^ p] for p in range(CHIPS)]))
        got = jnp.stack(got)
        cols = jnp.stack([at(got, chip ^ b) for b in range(CHIPS)])
        return jnp.moveaxis(cols, 0, -2).reshape(y.shape[0] * y.shape[1], -1)

    queries = (product(x_all, w_cols[:, 0]) + bias_cols[:, 0]).astype(BF)
    keys = product(x_all, w_cols[:, 1]).astype(BF)
    values = (product(x_all, w_cols[:, 2]) + bias_cols[:, 1]).astype(BF)
    cross_keys = product(m_all, w_cols[:, 4]).astype(BF)
    cross_values = (product(m_all, w_cols[:, 5]) + bias_cols[:, 4]).astype(BF)
    self_low, self_probs = attend(queries, keys, values, CHIPS, True)
    resid_one = x_all.astype(F32) + product(gather_columns(self_low), w_out[:, 0]) + attn_bias[:, 2]
    hidden_one, z_one, inv_one = layer_norm(resid_one, norm_gain[:, 0], norm_bias[:, 0])
    hidden_one_low = hidden_one.astype(BF)
    cross_queries = (product(hidden_one_low, w_cols[:, 3]) + bias_cols[:, 3]).astype(BF)
    cross_low, cross_probs = attend(cross_queries, cross_keys, cross_values, CHIPS, False)
    resid_two = hidden_one + product(gather_columns(cross_low), w_out[:, 1]) + attn_bias[:, 5]
    hidden_two, z_two, inv_two = layer_norm(resid_two, norm_gain[:, 1], norm_bias[:, 1])
    hidden_two_low = hidden_two.astype(BF)
    upward = product(hidden_two_low, w_up) + my_columns(bias_in)
    active, gelu_back = jax.vjp(exact_gelu, upward)
    active_low = active.astype(BF)
    branch = reduce_chips(product(active_low, w_down).reshape(CHIPS, length, width))
    resid_three = hidden_two[:length] + branch + bias_out
    hidden_three, z_three, inv_three = layer_norm(resid_three, norm_gain[:, 2], norm_bias[:, 2])
    final_low = hidden_three.astype(BF)

    vocab_rows = embedding.shape[0]
    plane = collect(final_low)
    plane = jnp.stack([plane, from_core(plane)]).reshape(TEAM, length, width)
    plane = across_teams(plane)
    questions = jnp.stack([(chip ^ k) * CORES + (core ^ d) for d in range(CORES) for k in range(CHIPS)])
    question_of = (jnp.arange(teams)[:, None] * TEAM + questions[None, :]).reshape(-1)
    if teams > 1:
        pass
    tokens = plane.reshape(-1, width)
    count = n_pb * length
    local_targets = targets - me * vocab_rows
    ids_here = local_targets[question_of].reshape(-1)
    scores = product_t(tokens, embedding)
    hit = ids_here[:, None] == jnp.arange(vocab_rows)[None, :]
    peak = jnp.max(scores, axis=1)
    total = jnp.sum(jnp.exp(scores - peak[:, None]), axis=1)
    block_norm = peak + jnp.log(total)
    block_pick = jnp.sum(jnp.where(hit, scores, 0.0), axis=1)
    place_of = jnp.argsort(question_of)
    stats = jnp.stack([block_norm, block_pick]).reshape(2, n_pb, length)[:, place_of]
    payload = jnp.concatenate([stats.reshape(-1), pad_mask[0].astype(F32), log_prior[0]])
    everyone = lax.all_to_all(
        jnp.broadcast_to(payload[None], (n_all, payload.shape[0])), ("slot", "pb"), 0, 0, tiled=True
    )
    split = 2 * n_pb * length
    got = everyone[:, :split].reshape(n_slot, n_pb, 2, n_pb, length)
    norms = jax.nn.logsumexp(got[:, :, 0], axis=1)
    picks = jnp.sum(got[:, :, 1], axis=1)
    masks = everyone[:n_pb, split : split + length]
    priors = everyone[:, split + length].reshape(n_slot, n_pb)
    usable = jnp.arange(n_slot)[:, None] < slot_counts[None, :]
    logp = picks - norms + priors[:, :, None]
    logp = jnp.where(usable[:, :, None], logp, -1e30)
    merged = jax.nn.logsumexp(logp, axis=0)
    token_grads = -masks[None] * jnp.where(usable[:, :, None], jnp.exp(logp - merged[None]), 0.0)
    token_logprob = at(merged, me)
    prior_grad = jnp.sum(at(at(token_grads, slot), me)).reshape(1, 1)

    def slot_view(values, s):
        return at(values, s)[question_of].reshape(-1)

    def logit_gradient(raw, is_hit, s):
        soft = jnp.exp(raw - slot_view(norms, s)[:, None])
        return (slot_view(token_grads, s)[:, None] * (jnp.where(is_hit, 1.0, 0.0) - soft)).astype(BF)

    logit_grad = logit_gradient(scores, hit, slot)
    partial = product(logit_grad, embedding).reshape(teams, TEAM, length, width)
    if teams > 1:
        partial = lax.psum_scatter(partial.astype(BF), "pb", axis_index_groups=team_groups(), tiled=False).astype(F32)
    else:
        partial = partial[0]
    pair = partial[:CHIPS] + from_core(partial[CHIPS:].astype(BF)).astype(F32)
    grad_final = reduce_chips(pair)

    grad_embedding = weight_product(logit_grad, tokens)
    for k in range(1, n_slot):
        others = from_slot(tokens, k)
        other_grad = logit_gradient(product_t(others, embedding), hit, (slot - k) % n_slot)
        grad_embedding = grad_embedding + weight_product(other_grad, others)

    dr_three, gain_three, shift_three = layer_norm_back(grad_final, z_three, inv_three, norm_gain[:, 2])
    e_three = dr_three.astype(BF)
    e_all = collect(e_three).reshape(-1, width)
    grad_down = weight_product(active_low, e_all)
    grad_active = product_t(e_all, w_down).astype(BF)
    grad_upward = gelu_back(grad_active.astype(F32))[0].astype(BF)
    grad_up = weight_product(hidden_two_low, grad_upward)
    sum_bias_in = jnp.sum(grad_upward.astype(F32), axis=0)
    dh_two = dr_three + reduce_chips(product_t(grad_upward, w_up).reshape(CHIPS, length, width))
    dr_two, gain_two, shift_two = layer_norm_back(dh_two, z_two[:length], inv_two[:length], norm_gain[:, 1])
    e_two = dr_two.astype(BF)
    e_all_two = collect(e_two).reshape(-1, width)
    grad_cross_out = weight_product(cross_low, e_all_two)
    grad_cross_mix = product_t(e_all_two, out_mine[:, 1]).astype(BF)
    dqc, dkc, dvc = attend_back(grad_cross_mix, cross_queries, cross_keys, cross_values, cross_probs, CHIPS)
    dh_one = dr_two + reduce_chips(product_t(dqc, w_cols[:, 3]).reshape(CHIPS, length, width))
    grad_passage = reduce_chips(
        (product_t(dkc, w_cols[:, 4]) + product_t(dvc, w_cols[:, 5])).reshape(CHIPS, -1, width)
    )
    dr_one, gain_one, shift_one = layer_norm_back(dh_one, z_one[:length], inv_one[:length], norm_gain[:, 0])
    e_one = dr_one.astype(BF)
    e_all_one = collect(e_one).reshape(-1, width)
    grad_self_out = weight_product(self_low, e_all_one)
    grad_self_mix = product_t(e_all_one, out_mine[:, 0]).astype(BF)
    dqs, dks, dvs = attend_back(grad_self_mix, queries, keys, values, self_probs, CHIPS)
    grad_source = dr_one + reduce_chips(
        (product_t(dqs, w_cols[:, 0]) + product_t(dks, w_cols[:, 1]) + product_t(dvs, w_cols[:, 2])).reshape(
            CHIPS, length, width
        )
    )

    slot_perm_up = lambda t: [(z, z + 1) for z in range(min(t, n_slot - 1))]
    slot_perm_down = lambda t: [(z, z - 1) for z in range(n_slot - 1, max(n_slot - 1 - t, 0), -1)]

    def reduce_slots(blocks):
        up = down = 0.0
        for t in range(1, n_slot):
            send = up + at(blocks, jnp.clip(n_slot - t + slot, 0, n_slot - 1))
            up = lax.ppermute(send.astype(BF), "slot", slot_perm_up(t)).astype(F32)
            send = down + at(blocks, jnp.clip(slot - n_slot + t, 0, n_slot - 1))
            down = lax.ppermute(send.astype(BF), "slot", slot_perm_down(t)).astype(F32)
        return at(blocks, slot) + up + down

    def reduce_core(blocks):
        return at(blocks, core) + from_core(at(blocks, 1 - core).astype(BF)).astype(F32)

    def over_teams(blocks):
        if teams == 1:
            return blocks[0]
        return lax.psum_scatter(blocks.astype(BF), "pb", axis_index_groups=team_groups(), tiled=False).astype(F32)

    def finish_columns(grad):
        cols = grad.shape[-1]
        rows = grad.shape[0] // n_all
        g = grad.reshape(n_slot, teams, CHIPS, CORES, rows, cols)
        g = over_teams(jnp.moveaxis(g, 1, 0))
        g = reduce_core(jnp.moveaxis(g, 2, 0))
        g = reduce_slots(g).astype(BF)
        got = [at(g, chip)] + [from_chip(at(g, chip ^ k), k) for k in range(1, CHIPS)]
        got = jnp.stack(got)
        ordered = jnp.stack([at(got, chip ^ b) for b in range(CHIPS)], axis=1)
        return ordered.reshape(rows, CHIPS * cols).astype(F32)

    def finish_rows(grad):
        rows = grad.shape[0] * CHIPS // n_all
        g = grad.reshape((teams, CHIPS, CORES, rows) + grad.shape[1:])
        g = over_teams(g)
        g = reduce_core(jnp.moveaxis(g, 1, 0))
        g = reduce_slots(g).astype(BF)
        pairs = []
        for s in range(n_slot):
            for i in range(n_pb):
                t, b, c = i // TEAM, (i % TEAM) // CORES, i % CORES
                pairs.append((s * n_pb + i, b * n_pb + t * TEAM + s * CORES + c))
        return lax.ppermute(g, ("slot", "pb"), pairs).astype(F32)

    out_up = finish_columns(grad_up)
    out_down = finish_rows(grad_down)
    out_cross = finish_rows(grad_cross_out)
    col_grads = [
        weight_product(hidden_one_low, dqc),
        weight_product(m_all, dkc),
        weight_product(m_all, dvc),
    ]
    out_cols_cross = [finish_columns(g) for g in col_grads]
    out_self = finish_rows(grad_self_out)
    out_cols_self = [finish_columns(weight_product(x_all, g)) for g in (dqs, dks, dvs)]
    out_attn = jnp.stack(out_cols_self + out_cols_cross, axis=1)
    out_outputs = jnp.stack([out_self, out_cross], axis=1)

    def spread(v):
        full = jnp.zeros((CHIPS, v.shape[0]), F32)
        return lax.dynamic_update_index_in_dim(full, v, chip, 0).reshape(-1)

    def total_rows(g):
        return jnp.sum(g.astype(F32), axis=0)

    small = jnp.stack(
        [
            spread(total_rows(dqs)),
            spread(total_rows(dvs)),
            total_rows(e_one),
            spread(total_rows(dqc)),
            spread(total_rows(dvc)),
            total_rows(e_two),
            gain_one,
            gain_two,
            gain_three,
            shift_one,
            shift_two,
            shift_three,
            total_rows(e_three),
        ]
    )
    rows = width // n_all
    small = jnp.moveaxis(small.reshape(-1, n_all, rows), 1, 0).reshape(n_all, -1)
    small = jnp.concatenate([small, spread(sum_bias_in).reshape(n_all, -1)], axis=1)
    small = jnp.sum(lax.all_to_all(small, ("slot", "pb"), 0, 0, tiled=True), axis=0)
    vectors = small[: 13 * rows].reshape(13, rows)
    return (
        token_logprob[None, :],
        grad_source[None, None],
        grad_passage[None, None],
        prior_grad,
        out_attn,
        out_outputs,
        out_up,
        out_down,
        vectors[:6].T,
        vectors[6:9].T,
        vectors[9:12].T,
        small[13 * rows :],
        vectors[12],
        grad_embedding,
    )


def solution(mesh):
    placed = (
        P("pb", "slot", None, None),
        P("pb", "slot", None, None),
        P("pb", None, None),
        P("pb", None, None),
        P("pb", None),
        P("pb", None),
        P(),
        P(),
        P(),
        P(),
        P(),
        P("pb", None),
        P(),
        P(),
        P("pb", None),
        P("pb", "slot"),
    )
    both = ("slot", "pb")
    return jax.shard_map(
        shards,
        mesh=mesh,
        in_specs=placed,
        out_specs=(
            P("pb", None),
            P("pb", "slot", None, None),
            P("pb", "slot", None, None),
            P("pb", "slot"),
            P(both, None, None),
            P(both, None, None),
            P(both, None),
            P(both, None),
            P(both, None),
            P(both, None),
            P(both, None),
            P(both),
            P(both),
            P("pb", None),
        ),
        check_vma=False,
    )
```

time: 2020 us -> 749 us (0.37)
  waiting for transfers between devices: 1650 us -> 145 us
  starting transfers between devices: 1.36 us -> 264 us
  blocking collectives: 87.1 us -> 0 us
  other arithmetic: 38 us -> 76.2 us
  local copies, waits for them, and re-layouts: 68.3 us -> 106 us
    reduce_scatter x5 -> x0, waiting for transfers between devices: 906 us -> none  [the longest x1 360 us: shards(): lax.psum_scatter(grad_attn, ('slot', 'pb'), scatter_dimension=0, tiled=True)]
    psum x1 -> x0, waiting for transfers between devices: 294 us -> none  [shards(): lax.psum(embed_part.astype(jnp.bfloat16), 'slot').astype(jnp.float32)]
    ppermute x0 -> x154, starting transfers between devices: none -> 255 us  [the longest x30 114 us: reduce_slots(): up = lax.ppermute(send.astype(BF), 'slot', slot_perm_up(t)).astype(F32)]
    unnamed x17 -> x0, waiting for transfers between devices: 243 us -> none
    all_gather x5 -> x0, waiting for transfers between devices: 209 us -> none  [the longest x1 68.1 us: shards(): lax.all_gather(attn_weight, 'pb', axis=0, tiled=True)]
    ppermute x0 -> x154, waiting for transfers between devices: none -> 138 us  [the longest x72 66 us: from_chip(): return lax.ppermute(x, 'pb', chip_pairs(lax.axis_size('pb'), k))]
    unnamed x3 -> x0, blocking collectives: 62.3 us -> none
    another operation x3 -> x42, other arithmetic: 5.52 us -> 31.9 us  [the longest x2 13.6 us: all_rows(): return natural(jnp.stack([mine, from_core(mine)]))]
  transfers between devices with their start and end apart: 14 -> 156, of which waited for: 13 -> 34; matrix products, arithmetic and copies ran while one was open for 8% -> 33% of each run, Pallas kernels for 0% -> 0%
where the time goes in v1:
time: 749 us; the launch traced here: 740 us
  starting transfers between devices  264 us (35%)
  waiting for transfers between devices  145 us (19%)
  matrix products  143 us (19%)
  local copies, waits for them, and re-layouts  106 us (14%)
  other arithmetic  76.2 us (10%)
    ppermute x30, starting transfers between devices, reduce_slots(): up = lax.ppermute(send.astype(BF), 'slot', slot_perm_up(t)).astype(F32)  114 us
    ppermute x72, starting transfers between devices, from_chip(): return lax.ppermute(x, 'pb', chip_pairs(lax.axis_size('pb'), k))  95.1 us
    dot_general x14, matrix products, weight_product(): return jnp.einsum('rd,re->de', a, g, preferred_element_type=F32)  82 us
    ppermute x72, waiting for transfers between devices, from_chip(): return lax.ppermute(x, 'pb', chip_pairs(lax.axis_size('pb'), k))  66 us
    ppermute x3, waiting for transfers between devices, from_slot(): return lax.ppermute(x, 'slot', [(i, (i + k) % size) for i in range(size)])  56.4 us
    ppermute x30, starting transfers between devices, reduce_slots(): down = lax.ppermute(send.astype(BF), 'slot', slot_perm_down(t)).astype(F32)  26.5 us
    dot_general x11, matrix products, product_t(): return jnp.einsum('re,de->rd', a, b, preferred_element_type=F32)  26.2 us
    dot_general x11, matrix products, product(): return jnp.dot(a, b, preferred_element_type=F32)  22.4 us
  transfers between devices with their start and end apart: 156, of which 34 were waited for; matrix products, arithmetic and copies ran while one was open for 33% of the time, Pallas kernels for 0%

profile of v1, /device:TPU:2, one launch (start us, length us, event | category | flops | bytes accessed | tf_op | source)
XLA Modules:
  0.0 740.2 jit_solution(15165734400888129849)
XLA Ops:
  51.5 28.8 %collective-permute-done.4 = bf16[1,128,6,256]{3,1,2,0:T(8,128)(2,1)S(1)} collective-permute-done((bf16[1,128,6,256]{3,1,2,0:T(8,128)(2,1)S(1)}, bf16[1,128,6,256]{3,1,2,0:T(8,128)(2,1)S(1)}, u32[]{:S(2)}, u32[]{:S(2)}) %collective-permute-start.4) | collective-permute-done | bytes 393248 | tf_op jit(solution)/shard_map/ppermute | solution.py:19
  110.9 8.9 %pad_maximum_fusion = bf16[2,4,1,128,2,1024]{5,4,3,1,2,0:T(2,128)(2,1)S(1)} fusion(bf16[1,4,1,128,2,1024]{5,4,3,1,2,0:T(2,128)(2,1)} %bitcast.41, bf16[1,4,1,128,2,1024]{5,4,3,1,2,0:T(2,128)(2,1)} %fusion.393), kind=kLoop, calls=%fused_computation.28 | loop fusion | flops 2097152 | bytes 8388608 | tf_op jit(solution)/shard_map/stack | solution.py:139
  173.5 7.6 %fusion.310 = (f32[512]{0:T(512)S(1)}, f32[512,4096]{1,0:T(8,128)S(1)}) fusion(bf16[512,1024]{1,0:T(8,128)(2,1)S(1)} %bitcast.1015, bf16[4096,1024]{1,0:T(8,128)(2,1)} %param.27), kind=kOutput, calls=%fused_computation.711 | convolution fusion | flops 4297063936 | bytes 17827840 | tf_op jit(solution)/shard_map/re,de->rd/dot_general | solution.py:41
  186.2 6.1 all-to-all-start
  192.3 6.9 all-to-all-done
  201.2 5.2 fusion.3
  206.5 8.4 %fusion.315 = f32[512,1024]{1,0:T(8,128)S(1)} fusion(bf16[512,4096]{1,0:T(8,128)(2,1)S(1)} %fusion.3, bf16[4096,1024]{1,0:T(8,128)(2,1)} %param.27), kind=kOutput, calls=%fused_computation.716 | convolution fusion | flops 4294967296 | bytes 14680064 | tf_op jit(solution)/shard_map/dot_general | solution.py:37
  236.7 8.2 %fusion.319 = f32[4096,1024]{1,0:T(8,128)} fusion(bf16[512,4096]{1,0:T(8,128)(2,1)S(1)} %copy-done.8, bf16[512,1024]{1,0:T(8,128)(2,1)S(1)} %bitcast.1019), kind=kOutput, calls=%fused_computation.720 | convolution fusion | flops 4294967296 | bytes 22020096 | tf_op jit(solution)/shard_map/rd,re->de/dot_general | solution.py:45
  263.3 56.4 %collective-permute-done.152 = bf16[512,1024]{1,0:T(8,128)(2,1)} collective-permute-done((bf16[512,1024]{1,0:T(8,128)(2,1)}, bf16[512,1024]{1,0:T(8,128)(2,1)}, u32[]{:S(2)}, u32[]{:S(2)}) %collective-permute-start.152) | collective-permute-done | bytes 1048608 | tf_op jit(solution)/shard_map/ppermute | solution.py:28
  321.7 17.5 %fusion.321 = f32[4096,1024]{1,0:T(8,128)} fusion(bf16[512,1024]{1,0:T(8,128)(2,1)} %collective-permute-done.152, bf16[4096,1024]{1,0:T(8,128)(2,1)} %param.27, f32[512]{0:T(512)} %sub.276, f32[512]{0:T(512)} %mul.415, s32[512]{0:T(512)S(1)} %eq.21), kind=kOutput, calls=%fused_computation.722 | convolution fusion | flops 8602517504 | bytes 26220544 | tf_op jit(solution)/shard_map/rd,re->de/dot_general | solution.py:45
  339.2 17.0 %fusion.320 = f32[4096,1024]{1,0:T(8,128)} fusion(bf16[512,1024]{1,0:T(8,128)(2,1)} %collective-permute-done.151, bf16[4096,1024]{1,0:T(8,128)(2,1)} %param.27, f32[512]{0:T(512)S(1)} %copy-done.109, f32[512]{0:T(512)} %mul.412, s32[512]{0:T(512)S(1)} %eq.21), kind=kOutput, calls=%fused_computation.721 | convolution fusion | flops 8602517504 | bytes 26220544 | tf_op jit(solution)/shard_map/rd,re->de/dot_general | solution.py:45
  356.1 31.3 %add_add_fusion = f32[4096,1024]{1,0:T(8,128)} fusion(f32[4096,1024]{1,0:T(8,128)} %fusion.321, f32[4096,1024]{1,0:T(8,128)} %fusion.319, f32[4096,1024]{1,0:T(8,128)} %fusion.320, bf16[512,1024]{1,0:T(8,128)(2,1)} %collective-permute-done.153, bf16[4096,1024]{1,0:T(8,128)(2,1)} %param.27, f32[512]{0:T(512)S(1)} %copy-done.108, f32[512]{0:T(512)S(1)} %copy-done.110, ...), kind=kOutput, calls=%fused_computation.12 | convolution fusion | flops 8615100416 | bytes 76552192 | tf_op jit(solution)/shard_map/rd,re->de/dot_general | solution.py:45
  388.5 5.8 convert_reduce_fusion
  533.1 5.2 collective-permute-start.109
  539.0 5.2 collective-permute-start.99
  544.9 5.2 collective-permute-start.90
  552.1 5.2 collective-permute-start.128
  617.5 5.2 collective-permute-start.69
  623.4 5.2 collective-permute-start.119
  635.9 5.2 collective-permute-start.60
  688.4 7.3 collective-permute-start.124
  698.1 7.5 %collective-permute-start.136 = (bf16[4,32,1024]{2,1,0:T(8,128)(2,1)S(1)}, bf16[4,32,1024]{2,1,0:T(8,128)(2,1)S(1)}, u32[]{:S(2)}, u32[]{:S(2)}) collective-permute-start(bf16[4,32,1024]{2,1,0:T(8,128)(2,1)S(1)} %get-tuple-element.137), channel_id=1, source_target_pairs={{0,8},{8,16},{16,24},{1,9},{9,17},{17,25},{2,10},{10,18},{18,26},{... | collective-permute-start | bytes 786440 | tf_op jit(solution)/shard_map/ppermute | solution.py:293
  716.0 8.1 %collective-permute-start.141 = (bf16[32,1024]{1,0:T(8,128)(2,1)S(1)}, bf16[32,1024]{1,0:T(8,128)(2,1)S(1)}, u32[]{:S(2)}, u32[]{:S(2)}) collective-permute-start(bf16[32,1024]{1,0:T(8,128)(2,1)S(1)} %get-tuple-element.239), channel_id=1, source_target_pairs={{0,4},{1,5},{2,6},{3,7},{4,0},{5,1},{6,2},{7,3},{8,12},{9,13},{10,... | collective-permute-start | bytes 196616 | tf_op jit(solution)/shard_map/ppermute | solution.py:19
  729.3 9.7 %collective-permute-done.150 = bf16[128,1024]{1,0:T(8,128)(2,1)S(1)} collective-permute-done((bf16[128,1024]{1,0:T(8,128)(2,1)S(1)}, bf16[128,1024]{1,0:T(8,128)(2,1)S(1)}, u32[]{:S(2)}, u32[]{:S(2)}) %collective-permute-start.150) | collective-permute-done | bytes 262176 | tf_op jit(solution)/shard_map/ppermute | solution.py:329
  (957 shorter events, 457.2 us)
Async XLA Ops:
  4.2 20.1 %collective-permute-start.16 = (bf16[128,1024]{1,0:T(8,128)(2,1)}, bf16[128,1024]{1,0:T(8,128)(2,1)}, u32[]{:S(2)}, u32[]{:S(2)}) collective-permute-start(bf16[128,1024]{1,0:T(8,128)(2,1)} %bitcast.1053), channel_id=1, source_target_pairs={{0,6},{1,7},{2,4},{3,5},{4,2},{5,3},{6,0},{7,1},{8,14},{9,15},{10,... | collective-permute-start | bytes 786440 | tf_op jit(solution)/shard_map/ppermute | solution.py:19
  5.7 20.2 %collective-permute-start.15 = (bf16[128,1024]{1,0:T(8,128)(2,1)}, bf16[128,1024]{1,0:T(8,128)(2,1)}, u32[]{:S(2)}, u32[]{:S(2)}) collective-permute-start(bf16[128,1024]{1,0:T(8,128)(2,1)} %bitcast.1054), channel_id=1, source_target_pairs={{0,4},{1,5},{2,6},{3,7},{4,0},{5,1},{6,2},{7,3},{8,12},{9,13},{10,... | collective-permute-start | bytes 786440 | tf_op jit(solution)/shard_map/ppermute | solution.py:19
  14.4 30.3 %collective-permute-start.3 = (bf16[1,128,6,256]{3,1,2,0:T(8,128)(2,1)S(1)}, bf16[1,128,6,256]{3,1,2,0:T(8,128)(2,1)S(1)}, u32[]{:S(2)}, u32[]{:S(2)}) collective-permute-start(bf16[1,128,6,256]{3,1,2,0:T(8,128)(2,1)S(1)} %bitcast.1042), channel_id=1, source_target_pairs={{0,2},{1,3},{2,0},{3,1},{4,6},{5,7},{6,4},{7,5},{8,10},{9,11},{10,... | collective-permute-start | bytes 1179656 | tf_op jit(solution)/shard_map/ppermute | solution.py:19
  32.8 48.3 %collective-permute-start.12 = (bf16[1,128,2,1024]{3,2,1,0:T(2,128)(2,1)S(1)}, bf16[1,128,2,1024]{3,2,1,0:T(2,128)(2,1)S(1)}, u32[]{:S(2)}, u32[]{:S(2)}) collective-permute-start(bf16[1,128,2,1024]{3,2,1,0:T(2,128)(2,1)S(1)} %bitcast.998), channel_id=1, source_target_pairs={{0,6},{1,7},{2,4},{3,5},{4,2},{5,3},{6,0},{7,1},{8,14},{9,15},{10,... | collective-permute-start | bytes 1572872 | tf_op jit(solution)/shard_map/ppermute | solution.py:19
  37.4 43.9 %collective-permute-start.11 = (bf16[1,128,2,1024]{3,2,1,0:T(2,128)(2,1)S(1)}, bf16[1,128,2,1024]{3,2,1,0:T(2,128)(2,1)S(1)}, u32[]{:S(2)}, u32[]{:S(2)}) collective-permute-start(bf16[1,128,2,1024]{3,2,1,0:T(2,128)(2,1)S(1)} %bitcast.999), channel_id=1, source_target_pairs={{0,4},{1,5},{2,6},{3,7},{4,0},{5,1},{6,2},{7,3},{8,12},{9,13},{10,... | collective-permute-start | bytes 1572872 | tf_op jit(solution)/shard_map/ppermute | solution.py:19
  38.9 42.4 %collective-permute-start.10 = (bf16[1,128,2,1024]{3,2,1,0:T(2,128)(2,1)S(1)}, bf16[1,128,2,1024]{3,2,1,0:T(2,128)(2,1)S(1)}, u32[]{:S(2)}, u32[]{:S(2)}) collective-permute-start(bf16[1,128,2,1024]{3,2,1,0:T(2,128)(2,1)S(1)} %bitcast.1000), channel_id=1, source_target_pairs={{0,2},{1,3},{2,0},{3,1},{4,6},{5,7},{6,4},{7,5},{8,10},{9,11},{10,... | collective-permute-start | bytes 1572872 | tf_op jit(solution)/shard_map/ppermute | solution.py:19
  44.1 36.2 %collective-permute-start.4 = (bf16[1,128,6,256]{3,1,2,0:T(8,128)(2,1)S(1)}, bf16[1,128,6,256]{3,1,2,0:T(8,128)(2,1)S(1)}, u32[]{:S(2)}, u32[]{:S(2)}) collective-permute-start(bf16[1,128,6,256]{3,1,2,0:T(8,128)(2,1)S(1)} %bitcast.1043), channel_id=1, source_target_pairs={{0,4},{1,5},{2,6},{3,7},{4,0},{5,1},{6,2},{7,3},{8,12},{9,13},{10,... | collective-permute-start | bytes 1179656 | tf_op jit(solution)/shard_map/ppermute | solution.py:19
  44.7 35.7 %collective-permute-start.5 = (bf16[1,128,6,256]{3,1,2,0:T(8,128)(2,1)}, bf16[1,128,6,256]{3,1,2,0:T(8,128)(2,1)S(1)}, u32[]{:S(2)}, u32[]{:S(2)}) collective-permute-start(bf16[1,128,6,256]{3,1,2,0:T(8,128)(2,1)} %bitcast.12), channel_id=1, source_target_pairs={{0,6},{1,7},{2,4},{3,5},{4,2},{5,3},{6,0},{7,1},{8,14},{9,15},{10,... | collective-permute-start | bytes 1179656 | tf_op jit(solution)/shard_map/ppermute | solution.py:19
  90.8 20.1 %collective-permute-start.13 = (bf16[4,1,128,2,1024]{4,3,2,1,0:T(2,128)(2,1)}, bf16[4,1,128,2,1024]{4,3,2,1,0:T(2,128)(2,1)}, u32[]{:S(2)}, u32[]{:S(2)}) collective-permute-start(bf16[4,1,128,2,1024]{4,3,2,1,0:T(2,128)(2,1)} %pad_maximum_fusion.2), channel_id=1, source_target_pairs={{0,1},{1,0},{2,3},{3,2},{4,5},{5,4},{6,7},{7,6},{8,9},{9,8},{10,11... | collective-permute-start | bytes 6291464 | tf_op jit(solution)/shard_map/ppermute | solution.py:23
  226.8 129.4 %collective-permute-start.153 = (bf16[512,1024]{1,0:T(8,128)(2,1)}, bf16[512,1024]{1,0:T(8,128)(2,1)}, u32[]{:S(2)}, u32[]{:S(2)}) collective-permute-start(bf16[512,1024]{1,0:T(8,128)(2,1)} %bitcast.1016), channel_id=1, source_target_pairs={{0,24},{8,0},{16,8},{24,16},{1,25},{9,1},{17,9},{25,17},{2,26},{10... | collective-permute-start | bytes 3145736 | tf_op jit(solution)/shard_map/ppermute | solution.py:28
  228.2 91.5 %collective-permute-start.152 = (bf16[512,1024]{1,0:T(8,128)(2,1)}, bf16[512,1024]{1,0:T(8,128)(2,1)}, u32[]{:S(2)}, u32[]{:S(2)}) collective-permute-start(bf16[512,1024]{1,0:T(8,128)(2,1)} %bitcast.1017), channel_id=1, source_target_pairs={{0,16},{8,24},{16,0},{24,8},{1,17},{9,25},{17,1},{25,9},{2,18},{10... | collective-permute-start | bytes 3145736 | tf_op jit(solution)/shard_map/ppermute | solution.py:28
  253.3 85.8 %collective-permute-start.151 = (bf16[512,1024]{1,0:T(8,128)(2,1)}, bf16[512,1024]{1,0:T(8,128)(2,1)}, u32[]{:S(2)}, u32[]{:S(2)}) collective-permute-start(bf16[512,1024]{1,0:T(8,128)(2,1)} %bitcast.1018), channel_id=1, source_target_pairs={{0,8},{8,16},{16,24},{24,0},{1,9},{9,17},{17,25},{25,1},{2,10},{10... | collective-permute-start | bytes 3145736 | tf_op jit(solution)/shard_map/ppermute | solution.py:28
  257.5 130.0 %collective-permute-start.38 = (bf16[64,1024]{1,0:T(8,128)(2,1)S(1)}, bf16[64,1024]{1,0:T(8,128)(2,1)S(1)}, u32[]{:S(2)}, u32[]{:S(2)}) collective-permute-start(bf16[64,1024]{1,0:T(8,128)(2,1)S(1)} %get-tuple-element.103), channel_id=1, source_target_pairs={{0,6},{1,7},{2,4},{3,5},{4,2},{5,3},{6,0},{7,1},{8,14},{9,15},{10,... | collective-permute-start | bytes 393224 | tf_op jit(solution)/shard_map/ppermute | solution.py:19
  259.0 128.4 %collective-permute-start.37 = (bf16[64,1024]{1,0:T(8,128)(2,1)S(1)}, bf16[64,1024]{1,0:T(8,128)(2,1)S(1)}, u32[]{:S(2)}, u32[]{:S(2)}) collective-permute-start(bf16[64,1024]{1,0:T(8,128)(2,1)S(1)} %get-tuple-element.103), channel_id=1, source_target_pairs={{0,4},{1,5},{2,6},{3,7},{4,0},{5,1},{6,2},{7,3},{8,12},{9,13},{10,... | collective-permute-start | bytes 393224 | tf_op jit(solution)/shard_map/ppermute | solution.py:19
  319.7 67.8 %collective-permute-start.36 = (bf16[64,1024]{1,0:T(8,128)(2,1)S(1)}, bf16[64,1024]{1,0:T(8,128)(2,1)}, u32[]{:S(2)}, u32[]{:S(2)}) collective-permute-start(bf16[64,1024]{1,0:T(8,128)(2,1)S(1)} %get-tuple-element.103), channel_id=1, source_target_pairs={{0,2},{1,3},{2,0},{3,1},{4,6},{5,7},{6,4},{7,5},{8,10},{9,11},{10,... | collective-permute-start | bytes 393224 | tf_op jit(solution)/shard_map/ppermute | solution.py:19
  402.3 272.2 %collective-permute-start.133 = (bf16[4,4,32,1024]{3,2,1,0:T(8,128)(2,1)}, bf16[4,4,32,1024]{3,2,1,0:T(8,128)(2,1)}, u32[]{:S(2)}, u32[]{:S(2)}) collective-permute-start(bf16[4,4,32,1024]{3,2,1,0:T(8,128)(2,1)} %fusion.45), channel_id=1, source_target_pairs={{0,1},{1,0},{2,3},{3,2},{4,5},{5,4},{6,7},{7,6},{8,9},{9,8},{10,11... | collective-permute-start | bytes 3145736 | tf_op jit(solution)/shard_map/ppermute | solution.py:23
  432.8 42.0 %collective-permute-start.87 = (bf16[4,4,32,256]{3,2,1,0:T(8,128)(2,1)}, bf16[4,4,32,256]{3,2,1,0:T(8,128)(2,1)}, u32[]{:S(2)}, u32[]{:S(2)}) collective-permute-start(bf16[4,4,32,256]{3,2,1,0:T(8,128)(2,1)} %fusion.92), channel_id=1, source_target_pairs={{0,1},{1,0},{2,3},{3,2},{4,5},{5,4},{6,7},{7,6},{8,9},{9,8},{10,11... | collective-permute-start | bytes 786440 | tf_op jit(solution)/shard_map/ppermute | solution.py:23
  460.4 30.9 %collective-permute-start.107 = (bf16[4,4,32,256]{3,2,1,0:T(8,128)(2,1)}, bf16[4,4,32,256]{3,2,1,0:T(8,128)(2,1)}, u32[]{:S(2)}, u32[]{:S(2)}) collective-permute-start(bf16[4,4,32,256]{3,2,1,0:T(8,128)(2,1)} %fusion.94), channel_id=1, source_target_pairs={{0,1},{1,0},{2,3},{3,2},{4,5},{5,4},{6,7},{7,6},{8,9},{9,8},{10,11... | collective-permute-start | bytes 786440 | tf_op jit(solution)/shard_map/ppermute | solution.py:23
  460.9 39.8 %collective-permute-start.97 = (bf16[4,4,32,256]{3,2,1,0:T(8,128)(2,1)}, bf16[4,4,32,256]{3,2,1,0:T(8,128)(2,1)}, u32[]{:S(2)}, u32[]{:S(2)}) collective-permute-start(bf16[4,4,32,256]{3,2,1,0:T(8,128)(2,1)} %fusion.93), channel_id=1, source_target_pairs={{0,1},{1,0},{2,3},{3,2},{4,5},{5,4},{6,7},{7,6},{8,9},{9,8},{10,11... | collective-permute-start | bytes 786440 | tf_op jit(solution)/shard_map/ppermute | solution.py:23
  474.8 27.4 %collective-permute-start.54 = (bf16[128,1024]{1,0:T(8,128)(2,1)}, bf16[128,1024]{1,0:T(8,128)(2,1)}, u32[]{:S(2)}, u32[]{:S(2)}) collective-permute-start(bf16[128,1024]{1,0:T(8,128)(2,1)} %get-tuple-element.151), channel_id=1, source_target_pairs={{0,2},{1,3},{2,0},{3,1},{4,6},{5,7},{6,4},{7,5},{8,10},{9,11},{10,... | collective-permute-start | bytes 786440 | tf_op jit(solution)/shard_map/ppermute | solution.py:19
  477.2 28.4 %collective-permute-start.56 = (bf16[128,1024]{1,0:T(8,128)(2,1)}, bf16[128,1024]{1,0:T(8,128)(2,1)}, u32[]{:S(2)}, u32[]{:S(2)}) collective-permute-start(bf16[128,1024]{1,0:T(8,128)(2,1)} %get-tuple-element.152), channel_id=1, source_target_pairs={{0,6},{1,7},{2,4},{3,5},{4,2},{5,3},{6,0},{7,1},{8,14},{9,15},{10,... | collective-permute-start | bytes 786440 | tf_op jit(solution)/shard_map/ppermute | solution.py:19
  498.0 60.0 %all-to-all-start.1 = ((f32[32,1,544]{2,1,0:T(1,128)}), f32[32,1,544]{2,1,0:T(1,128)S(1)}, u32[]{:S(2)}, u32[]{:S(2)}) async-start(f32[32,1,544]{2,1,0:T(1,128)} %copy.408), calls=%async_computation.1 | async-start | bytes 163840 | tf_op jit(solution)/shard_map/all_to_all | solution.py:372
  500.7 178.3 %collective-permute-start.143 = (bf16[4,128,1024]{2,1,0:T(8,128)(2,1)}, bf16[4,128,1024]{2,1,0:T(8,128)(2,1)}, u32[]{:S(2)}, u32[]{:S(2)}) collective-permute-start(bf16[4,128,1024]{2,1,0:T(8,128)(2,1)} %fusion.44), channel_id=1, source_target_pairs={{0,1},{1,0},{2,3},{3,2},{4,5},{5,4},{6,7},{7,6},{8,9},{9,8},{10,11... | collective-permute-start | bytes 3145736 | tf_op jit(solution)/shard_map/ppermute | solution.py:23
  670.2 35.4 %collective-permute-start.132 = (bf16[32,1024]{1,0:T(8,128)(2,1)S(1)}, bf16[32,1024]{1,0:T(8,128)(2,1)S(1)}, u32[]{:S(2)}, u32[]{:S(2)}) collective-permute-start(bf16[32,1024]{1,0:T(8,128)(2,1)S(1)} %fusion.143), channel_id=1, source_target_pairs={{0,0},{1,1},{2,8},{3,9},{4,16},{5,17},{6,24},{7,25},{8,2},{9,3},{1... | collective-permute-start | bytes 196616 | tf_op jit(solution)/shard_map/ppermute | solution.py:329
  (253 other events, 2743.9 us)
